TPU v7x, 256 devices: a whole 4x4x8 slice. The times are simulated.
256 devices in a mesh: row: 4 (over y), col: 16 (over z, core), layer: 4 (over x).
Axes of the slice: x: 4, y: 4, z: 8, core: 2. Of those that a mesh axis runs over, the one named last changes fastest.
Arguments:
- blocks: bfloat16 [5632, 128, 128], P(('col', 'layer')), may hold values from -6 to 6
- block_aux: int32 [5632], P(('col', 'layer')), may hold values from 0 to 23
- block_row: int32 [5632], P(('col', 'layer')), may hold values from 0 to 15, as said below
- block_col: int32 [5632], P(('col', 'layer')), may hold values from 0 to 159, as said below
- extents: int32 [5632], P(('col', 'layer')), may hold values from 32 to 128
- occ_green: bfloat16 [20480, 2048], P('layer', 'row'), may hold values from -0.00390625 to 0.00390625
- virt_green: bfloat16 [20480, 2048], P('layer', 'row'), may hold values from -0.00390625 to 0.00390625
Outputs:
- chi: float32 [24, 24], replicated
Inputs may be any that keep to these rules, and one draw needn't show every extreme that they name: block_row[n] numbers the block of 128 window functions that tile n covers. The owner of tile n is the pair (block_row[n], block_col[n] // 40). Within each device's share of 88 consecutive entries no owner appears more than 2 times, and one owner, the same for every share, appears exactly 2 times in every share.
All inputs are finite; a program needn't handle non-finite values.
Results may differ from a plain program's by a relative error of at most 0.0003.
Values may be sent and summed in bfloat16 or wider, within the bound.
No kernel may reach another device: no remote copies, remote signals or barrier semaphores. Data moves between devices by JAX's collectives and lax.ppermute only.
A program may use at most 192 MiB of HBM per device.

v0:
```python
import jax
import jax.numpy as jnp
from jax import lax
from jax.sharding import PartitionSpec as P

NP = 24


def on_device(blocks, block_aux, block_row, block_col, extents, occ_green, virt_green):
    row_count = lax.axis_size("row")
    col_count = lax.axis_size("col")
    layer_count = lax.axis_size("layer")
    held_count = blocks.shape[0]
    tile_side = blocks.shape[1]
    aux_count = NP
    owner_count = col_count * layer_count
    capacity = max(2, held_count // owner_count + 1)
    layer_blocks = occ_green.shape[0] // tile_side
    columns = jnp.arange(tile_side, dtype=jnp.int32)
    masked_tiles = jnp.where(
        columns[None, None, :] < extents[:, None, None], blocks, jnp.zeros((), blocks.dtype)
    )
    layer_of = block_col // layer_blocks
    target = block_row * layer_count + layer_of
    kept_col = block_col - layer_of * layer_blocks
    marked = (target[:, None] == jnp.arange(owner_count, dtype=jnp.int32)[None, :]).astype(
        jnp.int32
    )
    earlier = jnp.cumsum(marked, axis=0) - marked
    placed = target * capacity + jnp.sum(earlier * marked, axis=1)
    send_tiles = (
        jnp.zeros((owner_count * capacity, tile_side, tile_side), blocks.dtype)
        .at[placed]
        .set(masked_tiles)
    )
    send_meta = (
        jnp.zeros((owner_count * capacity, 2), jnp.int32)
        .at[placed]
        .set(jnp.stack([block_aux, kept_col], axis=1))
    )
    send_tiles = send_tiles.reshape(col_count, layer_count, capacity, tile_side, tile_side)
    send_meta = send_meta.reshape(col_count, layer_count, capacity, 2)
    total_slots = col_count * layer_count * capacity
    got_tiles, got_meta = (
        lax.all_to_all(
            send_tiles.reshape(total_slots, tile_side, tile_side),
            ("col", "layer"),
            split_axis=0,
            concat_axis=0,
            tiled=True,
        ),
        lax.all_to_all(
            send_meta.reshape(total_slots, 2),
            ("col", "layer"),
            split_axis=0,
            concat_axis=0,
            tiled=True,
        ),
    )
    group_size = col_count * capacity
    got_tiles = got_tiles.reshape(layer_count, group_size, tile_side, tile_side)
    got_meta = got_meta.reshape(layer_count, group_size, 2)
    occ_cols, virt_cols = (occ_green, virt_green)
    width_here = occ_cols.shape[1]
    offsets = jnp.arange(tile_side, dtype=jnp.int32)

    def add_group(totals, record):
        occ_total, virt_total = totals
        tile_group, meta_group = record
        row_index = meta_group[:, 1][:, None] * tile_side + offsets[None, :]
        occ_rows = occ_cols[row_index]
        virt_rows = virt_cols[row_index]
        occ_term = jnp.einsum(
            "gsv,gls->gvl", occ_rows, tile_group, preferred_element_type=jnp.float32
        )
        virt_term = jnp.einsum(
            "gvs,gsl->gvl", tile_group, virt_rows, preferred_element_type=jnp.float32
        )
        aux_index = meta_group[:, 0]
        return (
            (occ_total.at[aux_index].add(occ_term), virt_total.at[aux_index].add(virt_term)),
            None,
        )

    start_totals = (
        jnp.zeros((aux_count, width_here, tile_side), jnp.float32),
        jnp.zeros((aux_count, tile_side, width_here), jnp.float32),
    )
    (occ_total, virt_total), _ = lax.scan(add_group, start_totals, (got_tiles, got_meta))
    occ_done, virt_done = (
        lax.psum_scatter(occ_total, "layer", scatter_dimension=1, tiled=True),
        lax.psum_scatter(virt_total, "layer", scatter_dimension=2, tiled=True),
    )
    mesh_count = row_count * layer_count
    thin_rows = tile_side // mesh_count
    stack_count = mesh_count // col_count
    narrow = occ_done.shape[1]
    occ_five = occ_done.reshape(aux_count, 1, col_count, thin_rows, tile_side)
    virt_five = virt_done.reshape(aux_count, stack_count, col_count, thin_rows, narrow)
    occ_moved, virt_moved = (
        lax.all_to_all(occ_five, "col", split_axis=2, concat_axis=1, tiled=True),
        lax.all_to_all(virt_five, "col", split_axis=2, concat_axis=1, tiled=True),
    )
    virt_four = virt_moved.reshape(aux_count, mesh_count, thin_rows, narrow)
    virt_back = lax.all_to_all(virt_four, ("row", "layer"), split_axis=1, concat_axis=3, tiled=True)
    occ_final = occ_moved.reshape(aux_count, col_count, thin_rows, tile_side)
    virt_final = virt_back.reshape(aux_count, thin_rows, col_count, tile_side)
    chi_part = jnp.einsum(
        "pcji,qjci->pq",
        occ_final,
        virt_final,
        precision=lax.Precision.HIGHEST,
        preferred_element_type=jnp.float32,
    )
    return lax.psum(chi_part, ("row", "col", "layer"))


def solution(mesh):
    in_specs = (
        P(("col", "layer"), None, None),
        P(("col", "layer")),
        P(("col", "layer")),
        P(("col", "layer")),
        P(("col", "layer")),
        P("layer", "row"),
        P("layer", "row"),
    )
    out_specs = P()
    return jax.shard_map(
        on_device, mesh=mesh, in_specs=in_specs, out_specs=out_specs, check_vma=False
    )
```

profile of v0, /device:TPU:1, one launch (start us, length us, event | category | flops | bytes accessed | tf_op | source)
XLA Modules:
  0.0 813.1 jit_solution(16769600088540931036)
XLA Ops:
  11.0 13.0 %all-to-all-start = ((s32[64,2,2]{1,2,0:T(2,128)}), s32[64,2,2]{1,2,0:T(2,128)S(1)}, u32[]{:S(2)}, u32[]{:S(2)}) async-start(s32[64,2,2]{1,2,0:T(2,128)} %copy.19), calls=%async_computation | async-start | bytes 131072 | tf_op jit(solution)/shard_map/all_to_all | solution.py:52
  29.7 12.7 %scatter_fusion.2 = bf16[128,128,128]{2,1,0:T(8,128)(2,1)} fusion(bf16[128,128,128]{2,1,0:T(8,128)(2,1)} %broadcast_in_dim.41, s32[88]{0:T(128)S(1)} %compare_select_fusion.2, bf16[88,128,128]{2,1,0:T(8,128)(2,1)S(1)} %broadcast_select_fusion), kind=kCustom, calls=%fused_computation.5 | custom fusion | bytes 8651104 | tf_op jit(solution)/shard_map/scatter | solution.py:34
  42.4 10.4 %all-to-all-start.1 = ((bf16[128,128,128]{2,1,0:T(8,128)(2,1)}), bf16[128,128,128]{2,1,0:T(8,128)(2,1)}, u32[]{:S(2)}, u32[]{:S(2)}) async-start(bf16[128,128,128]{2,1,0:T(8,128)(2,1)} %scatter_fusion.2), calls=%async_computation.1 | async-start | bytes 8388608 | tf_op jit(solution)/shard_map/all_to_all | solution.py:45
  53.0 93.4 %all-to-all-done.1 = bf16[128,128,128]{2,1,0:T(8,128)(2,1)} async-done(((bf16[128,128,128]{2,1,0:T(8,128)(2,1)}), bf16[128,128,128]{2,1,0:T(8,128)(2,1)}, u32[]{:S(2)}, u32[]{:S(2)}) %all-to-all-start.1) | async-done | bytes 4194336 | tf_op jit(solution)/shard_map/all_to_all | solution.py:45
  153.2 366.1 %while.13 = (s32[]{:T(128)}, f32[24,512,128]{2,1,0:T(8,128)}, f32[24,128,512]{2,1,0:T(8,128)}, s32[4,32,2]{1,0,2:T(4,128)S(1)}, bf16[5120,512]{1,0:T(8,128)(2,1)...) while((s32[]{:T(128)}, f32[24,512,128]{2,1,0:T(8,128)}, ...), condition=%wide.region_7.8_spmd.clone, body=%wide.region_4.7_spmd.clone.sunk | while | flops 1077956736 | bytes 94423512 | solution.py:89
  153.3 20.6 %gather_fusion.1 = bf16[4096,512]{1,0:T(8,128)(2,1)} fusion(bf16[5120,512]{1,0:T(8,128)(2,1)} %get-tuple-element.167, s32[4096]{0:T(1024)S(1)} %fusion.37), kind=kCustom, calls=%fused_computation.1.clone.clone.1 | custom fusion | bytes 8404992 | tf_op jit(solution)/shard_map/while/body/eval_jaxpr/gather | solution.py:72
  173.8 7.0 fusion.39
  180.8 18.0 %scatter_fusion.1 = f32[24,128,512]{2,1,0:T(8,128)} fusion(f32[24,128,512]{2,1,0:T(8,128)} %get-tuple-element.155, s32[32]{0:T(128)S(1)} %get-tuple-element.143, f32[32,128,512]{2,1,0:T(8,128)} %fusion.39), kind=kCustom, calls=%fused_computation.3.clone.clone.1 | custom fusion | flops 2097152 | bytes 25165952 | tf_op jit(solution)/shard_map/while/body/eval_jaxpr/scatter-add | solution.py:81
  198.8 20.6 %gather_fusion = bf16[4096,512]{1,0:T(8,128)(2,1)} fusion(bf16[5120,512]{1,0:T(8,128)(2,1)} %get-tuple-element.165, s32[4096]{0:T(1024)S(1)} %fusion.37), kind=kCustom, calls=%fused_computation.clone.clone.1 | custom fusion | bytes 8404992 | tf_op jit(solution)/shard_map/while/body/eval_jaxpr/gather | solution.py:71
  219.3 7.0 fusion.38
  226.4 17.8 %scatter_fusion = f32[24,512,128]{2,1,0:T(8,128)} fusion(f32[24,512,128]{2,1,0:T(8,128)} %get-tuple-element.154, s32[32]{0:T(128)S(1)} %get-tuple-element.143, f32[32,512,128]{2,1,0:T(8,128)} %fusion.38), kind=kCustom, calls=%fused_computation.2.clone.clone.1 | custom fusion | flops 2097152 | bytes 25165952 | tf_op jit(solution)/shard_map/while/body/eval_jaxpr/scatter-add | solution.py:81
  244.3 20.6 %gather_fusion.1 = bf16[4096,512]{1,0:T(8,128)(2,1)} fusion(bf16[5120,512]{1,0:T(8,128)(2,1)} %get-tuple-element.167, s32[4096]{0:T(1024)S(1)} %fusion.37), kind=kCustom, calls=%fused_computation.1.clone.clone.1 | custom fusion | bytes 8404992 | tf_op jit(solution)/shard_map/while/body/eval_jaxpr/gather | solution.py:72
  271.8 18.1 %scatter_fusion.1 = f32[24,128,512]{2,1,0:T(8,128)} fusion(f32[24,128,512]{2,1,0:T(8,128)} %get-tuple-element.155, s32[32]{0:T(128)S(1)} %get-tuple-element.143, f32[32,128,512]{2,1,0:T(8,128)} %fusion.39), kind=kCustom, calls=%fused_computation.3.clone.clone.1 | custom fusion | flops 2097152 | bytes 25165952 | tf_op jit(solution)/shard_map/while/body/eval_jaxpr/scatter-add | solution.py:81
  289.9 20.6 %gather_fusion = bf16[4096,512]{1,0:T(8,128)(2,1)} fusion(bf16[5120,512]{1,0:T(8,128)(2,1)} %get-tuple-element.165, s32[4096]{0:T(1024)S(1)} %fusion.37), kind=kCustom, calls=%fused_computation.clone.clone.1 | custom fusion | bytes 8404992 | tf_op jit(solution)/shard_map/while/body/eval_jaxpr/gather | solution.py:71
  310.5 7.0 fusion.38
  317.5 18.1 %scatter_fusion = f32[24,512,128]{2,1,0:T(8,128)} fusion(f32[24,512,128]{2,1,0:T(8,128)} %get-tuple-element.154, s32[32]{0:T(128)S(1)} %get-tuple-element.143, f32[32,512,128]{2,1,0:T(8,128)} %fusion.38), kind=kCustom, calls=%fused_computation.2.clone.clone.1 | custom fusion | flops 2097152 | bytes 25165952 | tf_op jit(solution)/shard_map/while/body/eval_jaxpr/scatter-add | solution.py:81
  335.7 20.6 %gather_fusion.1 = bf16[4096,512]{1,0:T(8,128)(2,1)} fusion(bf16[5120,512]{1,0:T(8,128)(2,1)} %get-tuple-element.167, s32[4096]{0:T(1024)S(1)} %fusion.37), kind=kCustom, calls=%fused_computation.1.clone.clone.1 | custom fusion | bytes 8404992 | tf_op jit(solution)/shard_map/while/body/eval_jaxpr/gather | solution.py:72
  363.3 18.5 %scatter_fusion.1 = f32[24,128,512]{2,1,0:T(8,128)} fusion(f32[24,128,512]{2,1,0:T(8,128)} %get-tuple-element.155, s32[32]{0:T(128)S(1)} %get-tuple-element.143, f32[32,128,512]{2,1,0:T(8,128)} %fusion.39), kind=kCustom, calls=%fused_computation.3.clone.clone.1 | custom fusion | flops 2097152 | bytes 25165952 | tf_op jit(solution)/shard_map/while/body/eval_jaxpr/scatter-add | solution.py:81
  381.7 20.6 %gather_fusion = bf16[4096,512]{1,0:T(8,128)(2,1)} fusion(bf16[5120,512]{1,0:T(8,128)(2,1)} %get-tuple-element.165, s32[4096]{0:T(1024)S(1)} %fusion.37), kind=kCustom, calls=%fused_computation.clone.clone.1 | custom fusion | bytes 8404992 | tf_op jit(solution)/shard_map/while/body/eval_jaxpr/gather | solution.py:71
  402.3 7.0 fusion.38
  409.3 18.4 %scatter_fusion = f32[24,512,128]{2,1,0:T(8,128)} fusion(f32[24,512,128]{2,1,0:T(8,128)} %get-tuple-element.154, s32[32]{0:T(128)S(1)} %get-tuple-element.143, f32[32,512,128]{2,1,0:T(8,128)} %fusion.38), kind=kCustom, calls=%fused_computation.2.clone.clone.1 | custom fusion | flops 2097152 | bytes 25165952 | tf_op jit(solution)/shard_map/while/body/eval_jaxpr/scatter-add | solution.py:81
  427.8 20.6 %gather_fusion.1 = bf16[4096,512]{1,0:T(8,128)(2,1)} fusion(bf16[5120,512]{1,0:T(8,128)(2,1)} %get-tuple-element.167, s32[4096]{0:T(1024)S(1)} %fusion.37), kind=kCustom, calls=%fused_computation.1.clone.clone.1 | custom fusion | bytes 8404992 | tf_op jit(solution)/shard_map/while/body/eval_jaxpr/gather | solution.py:72
  455.4 18.1 %scatter_fusion.1 = f32[24,128,512]{2,1,0:T(8,128)} fusion(f32[24,128,512]{2,1,0:T(8,128)} %get-tuple-element.155, s32[32]{0:T(128)S(1)} %get-tuple-element.143, f32[32,128,512]{2,1,0:T(8,128)} %fusion.39), kind=kCustom, calls=%fused_computation.3.clone.clone.1 | custom fusion | flops 2097152 | bytes 25165952 | tf_op jit(solution)/shard_map/while/body/eval_jaxpr/scatter-add | solution.py:81
  473.5 20.6 %gather_fusion = bf16[4096,512]{1,0:T(8,128)(2,1)} fusion(bf16[5120,512]{1,0:T(8,128)(2,1)} %get-tuple-element.165, s32[4096]{0:T(1024)S(1)} %fusion.37), kind=kCustom, calls=%fused_computation.clone.clone.1 | custom fusion | bytes 8404992 | tf_op jit(solution)/shard_map/while/body/eval_jaxpr/gather | solution.py:71
  494.1 7.0 fusion.38
  501.1 18.2 %scatter_fusion = f32[24,512,128]{2,1,0:T(8,128)} fusion(f32[24,512,128]{2,1,0:T(8,128)} %get-tuple-element.154, s32[32]{0:T(128)S(1)} %get-tuple-element.143, f32[32,512,128]{2,1,0:T(8,128)} %fusion.38), kind=kCustom, calls=%fused_computation.2.clone.clone.1 | custom fusion | flops 2097152 | bytes 25165952 | tf_op jit(solution)/shard_map/while/body/eval_jaxpr/scatter-add | solution.py:81
  520.0 66.1 %reduce-scatter.5.cloned.1.call-done = f32[24,128,128]{2,1,0:T(8,128)} async-done(((f32[24,128,512]{2,1,0:T(8,128)}), f32[24,128,128]{2,1,0:T(8,128)}) %reduce-scatter.5.cloned.1.call-update) | async-done | bytes 1572880 | tf_op jit(solution)/shard_map/reduce_scatter | solution.py:92
  589.6 7.7 all-to-all-start.3
  597.2 57.7 %reduce-scatter.3.cloned.1.call-done = f32[24,128,128]{2,1,0:T(8,128)} async-done(((f32[24,512,128]{2,1,0:T(8,128)}), f32[24,128,128]{2,1,0:T(8,128)}) %reduce-scatter.3.cloned.1.call-update) | async-done | bytes 1572880 | tf_op jit(solution)/shard_map/reduce_scatter | solution.py:91
  657.3 47.2 %all_to_all.47 = f32[24,1,16,8,128]{4,0,3,1,2:T(8,128)S(1)} all-to-all(f32[24,1,16,8,128]{4,0,3,1,2:T(8,128)S(1)} %bitcast.69), channel_id=1, replica_groups=mesh['row'=4,'col'=16,'layer'=4] {'col'}, dimensions={2} | all-to-all | bytes 3145728 | tf_op jit(solution)/shard_map/all_to_all | solution.py:101
  704.5 27.5 %all_to_all.48 = f32[24,16,8,128]{3,0,2,1:T(8,128)S(1)} all-to-all(f32[24,16,8,128]{3,0,2,1:T(8,128)S(1)} %bitcast.68), channel_id=1, replica_groups=mesh['row'=4,'col'=16,'layer'=4] {'row','layer'}, dimensions={1} | all-to-all | bytes 3145728 | tf_op jit(solution)/shard_map/all_to_all | solution.py:105
  733.5 72.8 %psum.7 = f32[24,24]{1,0:T(8,128)} all-reduce(f32[24,24]{1,0:T(8,128)S(1)} %fusion.16), channel_id=1, replica_groups=mesh['row'=4,'col'=16,'layer'=4] {'row','col','layer'}, use_global_device_ids=true, to_apply=%region_10.11 | all-reduce | flops 576 | bytes 4608 | tf_op jit(solution)/shard_map/psum | solution.py:115
  (41 shorter events, 46.5 us)
Async XLA Ops:
  11.0 31.5 %all-to-all-start = ((s32[64,2,2]{1,2,0:T(2,128)}), s32[64,2,2]{1,2,0:T(2,128)S(1)}, u32[]{:S(2)}, u32[]{:S(2)}) async-start(s32[64,2,2]{1,2,0:T(2,128)} %copy.19), calls=%async_computation | async-start | bytes 131072 | tf_op jit(solution)/shard_map/all_to_all | solution.py:52
  42.4 103.9 %all-to-all-start.1 = ((bf16[128,128,128]{2,1,0:T(8,128)(2,1)}), bf16[128,128,128]{2,1,0:T(8,128)(2,1)}, u32[]{:S(2)}, u32[]{:S(2)}) async-start(bf16[128,128,128]{2,1,0:T(8,128)(2,1)} %scatter_fusion.2), calls=%async_computation.1 | async-start | bytes 8388608 | tf_op jit(solution)/shard_map/all_to_all | solution.py:45
  52.9 533.3 %reduce-scatter.5.cloned.1.call-start = ((), (), s32[]{:S(2)}) async-start(), calls=%async_computation.8 | async-start | bytes 7864320 | tf_op jit(solution)/shard_map/reduce_scatter | solution.py:92
  519.3 135.7 %reduce-scatter.3.cloned.1.call-start = ((), (), s32[]{:S(2)}) async-start(), calls=%async_computation.7 | async-start | bytes 7864320 | tf_op jit(solution)/shard_map/reduce_scatter | solution.py:91
  589.6 67.7 %all-to-all-start.3 = ((f32[24,1,16,8,128]{4,0,3,1,2:T(8,128)}), f32[24,1,16,8,128]{4,0,3,1,2:T(8,128)S(1)}, u32[]{:S(2)}, u32[]{:S(2)}) async-start(f32[24,1,16,8,128]{4,0,3,1,2:T(8,128)} %bitcast.6), calls=%async_computation.5 | async-start | bytes 3145728 | tf_op jit(solution)/shard_map/all_to_all | solution.py:102
Sparse Core Ops, SparseCore 0:
  519.4 66.6 reduce-scatter.4
  588.7 66.2 reduce-scatter.2
where the time goes:
time: 815 us; the launch traced here: 813 us
  waiting for transfers between devices  218 us (27%)
  local copies, waits for them, and re-layouts  195 us (24%)
  other arithmetic  151 us (19%)
  blocking collectives  147 us (18%)
  matrix products  57.5 us (7%)
  starting transfers between devices  31.3 us (4%)
  between operations  13.5 us (2%)
    all_to_all x1, waiting for transfers between devices, on_device(): lax.all_to_all(send_tiles.reshape(total_slots, tile_side, tile_side), ('c...  93.4 us
    gather x4, local copies, waits for them, and re-layouts, add_group(): virt_rows = virt_cols[row_index]  82.3 us
    gather x4, local copies, waits for them, and re-layouts, add_group(): occ_rows = occ_cols[row_index]  82.3 us
    psum x1, blocking collectives, on_device(): return lax.psum(chi_part, ('row', 'col', 'layer'))  72.8 us
    scatter-add x4, other arithmetic, add_group(): virt_total.at[aux_index].add(virt_term)  72.6 us
    scatter-add x4, other arithmetic, add_group(): occ_total.at[aux_index].add(occ_term)  72.5 us
    reduce_scatter x1, waiting for transfers between devices, on_device(): lax.psum_scatter(virt_total, 'layer', scatter_dimension=2, tiled=True)  66.1 us
    reduce_scatter x1, waiting for transfers between devices, on_device(): lax.psum_scatter(occ_total, 'layer', scatter_dimension=1, tiled=True)  57.7 us
  transfers between devices with their start and end apart: 5, of which 3 were waited for; matrix products, arithmetic and copies ran while one was open for 3% of the time, Pallas kernels for 0%

commit v1 on v0

--- a/solution.py
+++ b/solution.py
@@ -112,7 +112,7 @@
         precision=lax.Precision.HIGHEST,
         preferred_element_type=jnp.float32,
     )
-    return lax.psum(chi_part, ("row", "col", "layer"))
+    return jnp.sum(lax.all_gather(chi_part, ("row", "col", "layer")), axis=0)
 
 
 def solution(mesh):

time: 815 us -> 872 us (1.070)
  blocking collectives: 147 us -> 204 us
    all_gather x0 -> x1, blocking collectives: none -> 129 us  [on_device(): return jnp.sum(lax.all_gather(chi_part, ('row', 'col', 'layer')), axis=0)]
    psum x1 -> x0, blocking collectives: 72.8 us -> none  [on_device(): return lax.psum(chi_part, ('row', 'col', 'layer'))]
where the time goes in v1:
time: 872 us; the launch traced here: 871 us
  waiting for transfers between devices  218 us (25%)
  blocking collectives  204 us (23%)
  local copies, waits for them, and re-layouts  195 us (22%)
  other arithmetic  152 us (17%)
  matrix products  57.5 us (7%)
  starting transfers between devices  31.3 us (4%)
  between operations  13.5 us (2%)
    all_gather x1, blocking collectives, on_device(): return jnp.sum(lax.all_gather(chi_part, ('row', 'col', 'layer')), axis=0)  129 us
    all_to_all x1, waiting for transfers between devices, on_device(): lax.all_to_all(send_tiles.reshape(total_slots, tile_side, tile_side), ('c...  93.4 us
    gather x4, local copies, waits for them, and re-layouts, add_group(): virt_rows = virt_cols[row_index]  82.3 us
    gather x4, local copies, waits for them, and re-layouts, add_group(): occ_rows = occ_cols[row_index]  82.3 us
    scatter-add x4, other arithmetic, add_group(): virt_total.at[aux_index].add(virt_term)  72.6 us
    scatter-add x4, other arithmetic, add_group(): occ_total.at[aux_index].add(occ_term)  72.5 us
    reduce_scatter x1, waiting for transfers between devices, on_device(): lax.psum_scatter(virt_total, 'layer', scatter_dimension=2, tiled=True)  66.1 us
    reduce_scatter x1, waiting for transfers between devices, on_device(): lax.psum_scatter(occ_total, 'layer', scatter_dimension=1, tiled=True)  57.7 us
  transfers between devices with their start and end apart: 5, of which 3 were waited for; matrix products, arithmetic and copies ran while one was open for 3% of the time, Pallas kernels for 0%

profile of v1, /device:TPU:1, one launch (start us, length us, event | category | flops | bytes accessed | tf_op | source)
XLA Modules:
  0.0 870.5 jit_solution(16094583937185909920)
XLA Ops:
  11.0 13.0 %all-to-all-start = ((s32[64,2,2]{1,2,0:T(2,128)}), s32[64,2,2]{1,2,0:T(2,128)S(1)}, u32[]{:S(2)}, u32[]{:S(2)}) async-start(s32[64,2,2]{1,2,0:T(2,128)} %copy.19), calls=%async_computation | async-start | bytes 131072 | tf_op jit(solution)/shard_map/all_to_all | solution.py:52
  29.7 12.7 %scatter_fusion.2 = bf16[128,128,128]{2,1,0:T(8,128)(2,1)} fusion(bf16[128,128,128]{2,1,0:T(8,128)(2,1)} %broadcast_in_dim.41, s32[88]{0:T(128)S(1)} %compare_select_fusion.2, bf16[88,128,128]{2,1,0:T(8,128)(2,1)S(1)} %broadcast_select_fusion), kind=kCustom, calls=%fused_computation.5 | custom fusion | bytes 8651104 | tf_op jit(solution)/shard_map/scatter | solution.py:34
  42.4 10.4 %all-to-all-start.1 = ((bf16[128,128,128]{2,1,0:T(8,128)(2,1)}), bf16[128,128,128]{2,1,0:T(8,128)(2,1)}, u32[]{:S(2)}, u32[]{:S(2)}) async-start(bf16[128,128,128]{2,1,0:T(8,128)(2,1)} %scatter_fusion.2), calls=%async_computation.1 | async-start | bytes 8388608 | tf_op jit(solution)/shard_map/all_to_all | solution.py:45
  53.0 93.4 %all-to-all-done.1 = bf16[128,128,128]{2,1,0:T(8,128)(2,1)} async-done(((bf16[128,128,128]{2,1,0:T(8,128)(2,1)}), bf16[128,128,128]{2,1,0:T(8,128)(2,1)}, u32[]{:S(2)}, u32[]{:S(2)}) %all-to-all-start.1) | async-done | bytes 4194336 | tf_op jit(solution)/shard_map/all_to_all | solution.py:45
  153.2 366.1 %while.13 = (s32[]{:T(128)}, f32[24,512,128]{2,1,0:T(8,128)}, f32[24,128,512]{2,1,0:T(8,128)}, s32[4,32,2]{1,0,2:T(4,128)S(1)}, bf16[5120,512]{1,0:T(8,128)(2,1)...) while((s32[]{:T(128)}, f32[24,512,128]{2,1,0:T(8,128)}, ...), condition=%wide.region_7.8_spmd.clone, body=%wide.region_4.7_spmd.clone.sunk | while | flops 1077956736 | bytes 94423512 | solution.py:89
  153.3 20.6 %gather_fusion.1 = bf16[4096,512]{1,0:T(8,128)(2,1)} fusion(bf16[5120,512]{1,0:T(8,128)(2,1)} %get-tuple-element.167, s32[4096]{0:T(1024)S(1)} %fusion.37), kind=kCustom, calls=%fused_computation.1.clone.clone.1 | custom fusion | bytes 8404992 | tf_op jit(solution)/shard_map/while/body/eval_jaxpr/gather | solution.py:72
  173.8 7.0 fusion.39
  180.8 18.0 %scatter_fusion.1 = f32[24,128,512]{2,1,0:T(8,128)} fusion(f32[24,128,512]{2,1,0:T(8,128)} %get-tuple-element.155, s32[32]{0:T(128)S(1)} %get-tuple-element.143, f32[32,128,512]{2,1,0:T(8,128)} %fusion.39), kind=kCustom, calls=%fused_computation.3.clone.clone.1 | custom fusion | flops 2097152 | bytes 25165952 | tf_op jit(solution)/shard_map/while/body/eval_jaxpr/scatter-add | solution.py:81
  198.8 20.6 %gather_fusion = bf16[4096,512]{1,0:T(8,128)(2,1)} fusion(bf16[5120,512]{1,0:T(8,128)(2,1)} %get-tuple-element.165, s32[4096]{0:T(1024)S(1)} %fusion.37), kind=kCustom, calls=%fused_computation.clone.clone.1 | custom fusion | bytes 8404992 | tf_op jit(solution)/shard_map/while/body/eval_jaxpr/gather | solution.py:71
  219.3 7.0 fusion.38
  226.4 17.8 %scatter_fusion = f32[24,512,128]{2,1,0:T(8,128)} fusion(f32[24,512,128]{2,1,0:T(8,128)} %get-tuple-element.154, s32[32]{0:T(128)S(1)} %get-tuple-element.143, f32[32,512,128]{2,1,0:T(8,128)} %fusion.38), kind=kCustom, calls=%fused_computation.2.clone.clone.1 | custom fusion | flops 2097152 | bytes 25165952 | tf_op jit(solution)/shard_map/while/body/eval_jaxpr/scatter-add | solution.py:81
  244.3 20.6 %gather_fusion.1 = bf16[4096,512]{1,0:T(8,128)(2,1)} fusion(bf16[5120,512]{1,0:T(8,128)(2,1)} %get-tuple-element.167, s32[4096]{0:T(1024)S(1)} %fusion.37), kind=kCustom, calls=%fused_computation.1.clone.clone.1 | custom fusion | bytes 8404992 | tf_op jit(solution)/shard_map/while/body/eval_jaxpr/gather | solution.py:72
  271.8 18.1 %scatter_fusion.1 = f32[24,128,512]{2,1,0:T(8,128)} fusion(f32[24,128,512]{2,1,0:T(8,128)} %get-tuple-element.155, s32[32]{0:T(128)S(1)} %get-tuple-element.143, f32[32,128,512]{2,1,0:T(8,128)} %fusion.39), kind=kCustom, calls=%fused_computation.3.clone.clone.1 | custom fusion | flops 2097152 | bytes 25165952 | tf_op jit(solution)/shard_map/while/body/eval_jaxpr/scatter-add | solution.py:81
  289.9 20.6 %gather_fusion = bf16[4096,512]{1,0:T(8,128)(2,1)} fusion(bf16[5120,512]{1,0:T(8,128)(2,1)} %get-tuple-element.165, s32[4096]{0:T(1024)S(1)} %fusion.37), kind=kCustom, calls=%fused_computation.clone.clone.1 | custom fusion | bytes 8404992 | tf_op jit(solution)/shard_map/while/body/eval_jaxpr/gather | solution.py:71
  310.5 7.0 fusion.38
  317.5 18.1 %scatter_fusion = f32[24,512,128]{2,1,0:T(8,128)} fusion(f32[24,512,128]{2,1,0:T(8,128)} %get-tuple-element.154, s32[32]{0:T(128)S(1)} %get-tuple-element.143, f32[32,512,128]{2,1,0:T(8,128)} %fusion.38), kind=kCustom, calls=%fused_computation.2.clone.clone.1 | custom fusion | flops 2097152 | bytes 25165952 | tf_op jit(solution)/shard_map/while/body/eval_jaxpr/scatter-add | solution.py:81
  335.7 20.6 %gather_fusion.1 = bf16[4096,512]{1,0:T(8,128)(2,1)} fusion(bf16[5120,512]{1,0:T(8,128)(2,1)} %get-tuple-element.167, s32[4096]{0:T(1024)S(1)} %fusion.37), kind=kCustom, calls=%fused_computation.1.clone.clone.1 | custom fusion | bytes 8404992 | tf_op jit(solution)/shard_map/while/body/eval_jaxpr/gather | solution.py:72
  363.3 18.5 %scatter_fusion.1 = f32[24,128,512]{2,1,0:T(8,128)} fusion(f32[24,128,512]{2,1,0:T(8,128)} %get-tuple-element.155, s32[32]{0:T(128)S(1)} %get-tuple-element.143, f32[32,128,512]{2,1,0:T(8,128)} %fusion.39), kind=kCustom, calls=%fused_computation.3.clone.clone.1 | custom fusion | flops 2097152 | bytes 25165952 | tf_op jit(solution)/shard_map/while/body/eval_jaxpr/scatter-add | solution.py:81
  381.7 20.6 %gather_fusion = bf16[4096,512]{1,0:T(8,128)(2,1)} fusion(bf16[5120,512]{1,0:T(8,128)(2,1)} %get-tuple-element.165, s32[4096]{0:T(1024)S(1)} %fusion.37), kind=kCustom, calls=%fused_computation.clone.clone.1 | custom fusion | bytes 8404992 | tf_op jit(solution)/shard_map/while/body/eval_jaxpr/gather | solution.py:71
  402.3 7.0 fusion.38
  409.3 18.4 %scatter_fusion = f32[24,512,128]{2,1,0:T(8,128)} fusion(f32[24,512,128]{2,1,0:T(8,128)} %get-tuple-element.154, s32[32]{0:T(128)S(1)} %get-tuple-element.143, f32[32,512,128]{2,1,0:T(8,128)} %fusion.38), kind=kCustom, calls=%fused_computation.2.clone.clone.1 | custom fusion | flops 2097152 | bytes 25165952 | tf_op jit(solution)/shard_map/while/body/eval_jaxpr/scatter-add | solution.py:81
  427.8 20.6 %gather_fusion.1 = bf16[4096,512]{1,0:T(8,128)(2,1)} fusion(bf16[5120,512]{1,0:T(8,128)(2,1)} %get-tuple-element.167, s32[4096]{0:T(1024)S(1)} %fusion.37), kind=kCustom, calls=%fused_computation.1.clone.clone.1 | custom fusion | bytes 8404992 | tf_op jit(solution)/shard_map/while/body/eval_jaxpr/gather | solution.py:72
  455.4 18.1 %scatter_fusion.1 = f32[24,128,512]{2,1,0:T(8,128)} fusion(f32[24,128,512]{2,1,0:T(8,128)} %get-tuple-element.155, s32[32]{0:T(128)S(1)} %get-tuple-element.143, f32[32,128,512]{2,1,0:T(8,128)} %fusion.39), kind=kCustom, calls=%fused_computation.3.clone.clone.1 | custom fusion | flops 2097152 | bytes 25165952 | tf_op jit(solution)/shard_map/while/body/eval_jaxpr/scatter-add | solution.py:81
  473.5 20.6 %gather_fusion = bf16[4096,512]{1,0:T(8,128)(2,1)} fusion(bf16[5120,512]{1,0:T(8,128)(2,1)} %get-tuple-element.165, s32[4096]{0:T(1024)S(1)} %fusion.37), kind=kCustom, calls=%fused_computation.clone.clone.1 | custom fusion | bytes 8404992 | tf_op jit(solution)/shard_map/while/body/eval_jaxpr/gather | solution.py:71
  494.1 7.0 fusion.38
  501.1 18.2 %scatter_fusion = f32[24,512,128]{2,1,0:T(8,128)} fusion(f32[24,512,128]{2,1,0:T(8,128)} %get-tuple-element.154, s32[32]{0:T(128)S(1)} %get-tuple-element.143, f32[32,512,128]{2,1,0:T(8,128)} %fusion.38), kind=kCustom, calls=%fused_computation.2.clone.clone.1 | custom fusion | flops 2097152 | bytes 25165952 | tf_op jit(solution)/shard_map/while/body/eval_jaxpr/scatter-add | solution.py:81
  520.0 66.1 %reduce-scatter.5.cloned.1.call-done = f32[24,128,128]{2,1,0:T(8,128)} async-done(((f32[24,128,512]{2,1,0:T(8,128)}), f32[24,128,128]{2,1,0:T(8,128)}) %reduce-scatter.5.cloned.1.call-update) | async-done | bytes 1572880 | tf_op jit(solution)/shard_map/reduce_scatter | solution.py:92
  589.6 7.7 all-to-all-start.3
  597.2 57.7 %reduce-scatter.3.cloned.1.call-done = f32[24,128,128]{2,1,0:T(8,128)} async-done(((f32[24,512,128]{2,1,0:T(8,128)}), f32[24,128,128]{2,1,0:T(8,128)}) %reduce-scatter.3.cloned.1.call-update) | async-done | bytes 1572880 | tf_op jit(solution)/shard_map/reduce_scatter | solution.py:91
  657.3 47.2 %all_to_all.47 = f32[24,1,16,8,128]{4,0,3,1,2:T(8,128)S(1)} all-to-all(f32[24,1,16,8,128]{4,0,3,1,2:T(8,128)S(1)} %bitcast.71), channel_id=1, replica_groups=mesh['row'=4,'col'=16,'layer'=4] {'col'}, dimensions={2} | all-to-all | bytes 3145728 | tf_op jit(solution)/shard_map/all_to_all | solution.py:101
  704.5 27.5 %all_to_all.48 = f32[24,16,8,128]{3,0,2,1:T(8,128)S(1)} all-to-all(f32[24,16,8,128]{3,0,2,1:T(8,128)S(1)} %bitcast.70), channel_id=1, replica_groups=mesh['row'=4,'col'=16,'layer'=4] {'row','layer'}, dimensions={1} | all-to-all | bytes 3145728 | tf_op jit(solution)/shard_map/all_to_all | solution.py:105
  733.5 129.3 %all-gather = f32[6144,24]{1,0:T(8,128)S(1)} all-gather(f32[24,24]{1,0:T(8,128)S(1)} %fusion.16), channel_id=2, replica_groups=mesh['row'=4,'col'=16,'layer'=4] {'row','col','layer'}, dimensions={0}, use_global_device_ids=true | all-gather | bytes 592128 | tf_op jit(solution)/shard_map/all_gather | solution.py:115
  (42 shorter events, 47.4 us)
Async XLA Ops:
  11.0 31.5 %all-to-all-start = ((s32[64,2,2]{1,2,0:T(2,128)}), s32[64,2,2]{1,2,0:T(2,128)S(1)}, u32[]{:S(2)}, u32[]{:S(2)}) async-start(s32[64,2,2]{1,2,0:T(2,128)} %copy.19), calls=%async_computation | async-start | bytes 131072 | tf_op jit(solution)/shard_map/all_to_all | solution.py:52
  42.4 103.9 %all-to-all-start.1 = ((bf16[128,128,128]{2,1,0:T(8,128)(2,1)}), bf16[128,128,128]{2,1,0:T(8,128)(2,1)}, u32[]{:S(2)}, u32[]{:S(2)}) async-start(bf16[128,128,128]{2,1,0:T(8,128)(2,1)} %scatter_fusion.2), calls=%async_computation.1 | async-start | bytes 8388608 | tf_op jit(solution)/shard_map/all_to_all | solution.py:45
  52.9 533.3 %reduce-scatter.5.cloned.1.call-start = ((), (), s32[]{:S(2)}) async-start(), calls=%async_computation.8 | async-start | bytes 7864320 | tf_op jit(solution)/shard_map/reduce_scatter | solution.py:92
  519.3 135.7 %reduce-scatter.3.cloned.1.call-start = ((), (), s32[]{:S(2)}) async-start(), calls=%async_computation.7 | async-start | bytes 7864320 | tf_op jit(solution)/shard_map/reduce_scatter | solution.py:91
  589.6 67.7 %all-to-all-start.3 = ((f32[24,1,16,8,128]{4,0,3,1,2:T(8,128)}), f32[24,1,16,8,128]{4,0,3,1,2:T(8,128)S(1)}, u32[]{:S(2)}, u32[]{:S(2)}) async-start(f32[24,1,16,8,128]{4,0,3,1,2:T(8,128)} %bitcast.6), calls=%async_computation.5 | async-start | bytes 3145728 | tf_op jit(solution)/shard_map/all_to_all | solution.py:102
Sparse Core Ops, SparseCore 0:
  519.4 66.6 reduce-scatter.4
  588.7 66.2 reduce-scatter.2
